TPU v7x, 128 devices: a whole 4x4x4 slice. The times are simulated.
128 devices in a mesh: dp: 16 (over z, y), ctx: 8 (over x, core).
Axes of the slice: x: 4, y: 4, z: 4, core: 2. Of those that a mesh axis runs over, the one named last changes fastest.
Arguments:
- hidden_in: bfloat16 [16384, 960], P(('dp', 'ctx')), may hold values from -6 to 6
- out_grad: bfloat16 [16384, 960], P(('dp', 'ctx')), may hold values from -6 to 6
- norm_gains: bfloat16 [2, 960], P(None, 'dp'), may hold values from 0.5 to 1.5
- q_weight: bfloat16 [960, 960], P('dp'), may hold values from -0.1875 to 0.1875
- k_weight: bfloat16 [960, 320], P('dp'), may hold values from -0.1875 to 0.1875
- v_weight: bfloat16 [960, 320], P('dp'), may hold values from -0.1875 to 0.1875
- out_weight: bfloat16 [960, 960], P('dp'), may hold values from -0.75 to 0.75
- gate_weight: bfloat16 [960, 2560], P('dp'), may hold values from -0.1875 to 0.1875
- up_weight: bfloat16 [960, 2560], P('dp'), may hold values from -0.1875 to 0.1875
- down_weight: bfloat16 [960, 2560], P('dp'), may hold values from -0.125 to 0.125
Outputs:
- hidden_out: bfloat16 [16384, 960], P(('dp', 'ctx'))
- in_grad: float32 [16384, 960], P(('dp', 'ctx'))
- gains_grad: float32 [2, 960], P(None, 'dp')
- q_weight_grad: float32 [960, 960], P('dp')
- k_weight_grad: float32 [960, 320], P('dp')
- v_weight_grad: float32 [960, 320], P('dp')
- out_weight_grad: float32 [960, 960], P('dp')
- gate_weight_grad: float32 [960, 2560], P('dp')
- up_weight_grad: float32 [960, 2560], P('dp')
- down_weight_grad: float32 [960, 2560], P('dp')
All inputs are finite; a program needn't handle non-finite values.
Results may differ from a plain program's by a relative error of at most 0.015.
Values may be sent and summed in bfloat16 or wider, within the bound.
No kernel may reach another device: no remote copies, remote signals or barrier semaphores. Data moves between devices by JAX's collectives and lax.ppermute only.
A program may use at most 192 MiB of HBM per device.

v0:
```python
import math
import jax
import jax.numpy as jnp
from jax import lax
from jax.sharding import PartitionSpec as P

HEADS = 15
KV_HEADS = 5
HEAD_DIM = 64
EPS = 1e-05
ROPE_BASE = 100000.0
NEG_FILL = -1e30


def passed_along(block, axis, distance):
    devices = range(lax.axis_size(axis))
    route = [((i - distance) % len(devices), i) for i in devices]
    return lax.ppermute(block, axis, route)


def shifted(block, axis, distance):
    devices = range(lax.axis_size(axis))
    route = [(i - distance, i) for i in devices if i - distance in devices]
    return lax.ppermute(block, axis, route)


def rotary(positions, head_size):
    half = head_size // 2
    freq = ROPE_BASE ** (-(jnp.arange(half, dtype=jnp.float32) * 2.0) / head_size)
    angles = positions[:, None] * freq[None, :]
    return (
        jnp.concatenate([jnp.cos(angles), jnp.cos(angles)], axis=1),
        jnp.concatenate([jnp.sin(angles), jnp.sin(angles)], axis=1),
    )


def rotate(values, cosine, sine, sign):
    half = values.shape[-1] // 2
    turned = jnp.concatenate([-values[..., half:], values[..., :half]], axis=-1)
    return values * cosine[:, None, :] + sign * turned * sine[:, None, :]


def norm_forward(values):
    scale = lax.rsqrt(jnp.mean(values * values, axis=1, keepdims=True) + EPS)
    return (values * scale, scale)


def norm_backward(grad_normed, normed, scale, gain):
    weighted = grad_normed * gain
    inner = jnp.mean(weighted * normed, axis=1, keepdims=True)
    return (scale * (weighted - normed * inner), jnp.sum(grad_normed * normed, axis=0))


def contract_rows(left, right):
    return lax.dot_general(
        left, right, (((0,), (0,)), ((), ())), preferred_element_type=jnp.float32
    )


def contract_cols(left, right):
    return lax.dot_general(
        left, right, (((1,), (1,)), ((), ())), preferred_element_type=jnp.float32
    )


def on_device(
    hidden_in,
    out_grad,
    norm_gains,
    q_weight,
    k_weight,
    v_weight,
    out_weight,
    gate_weight,
    up_weight,
    down_weight,
):
    rows = hidden_in.shape[0]
    ctx_count = lax.axis_size("ctx")
    ctx_index = lax.axis_index("ctx")
    groups = HEADS // KV_HEADS
    kv_width = KV_HEADS * HEAD_DIM
    scaling = 1.0 / math.sqrt(HEAD_DIM)
    shards = (
        norm_gains,
        q_weight,
        k_weight,
        v_weight,
        out_weight,
        gate_weight,
        up_weight,
        down_weight,
    )
    gathered = (
        lax.all_gather(shards[0], "dp", axis=1, tiled=True),
        lax.all_gather(shards[1], "dp", axis=0, tiled=True),
        lax.all_gather(shards[2], "dp", axis=0, tiled=True),
        lax.all_gather(shards[3], "dp", axis=0, tiled=True),
        lax.all_gather(shards[4], "dp", axis=0, tiled=True),
        lax.all_gather(shards[5], "dp", axis=0, tiled=True),
        lax.all_gather(shards[6], "dp", axis=0, tiled=True),
        lax.all_gather(shards[7], "dp", axis=0, tiled=True),
    )
    gain_rows, query_mat, key_mat, value_mat, output_mat, gate_mat, up_mat, down_mat = gathered
    gain_first = gain_rows[0].astype(jnp.float32)
    gain_second = gain_rows[1].astype(jnp.float32)
    query_pos = ctx_index * rows + jnp.arange(rows, dtype=jnp.int32)
    cosine, sine = rotary(query_pos.astype(jnp.float32), HEAD_DIM)
    inputs_wide = hidden_in.astype(jnp.float32)
    normed_one, scale_one = norm_forward(inputs_wide)
    first_in = (normed_one * gain_first).astype(jnp.bfloat16)
    queries = jnp.dot(first_in, query_mat, preferred_element_type=jnp.float32).reshape(
        rows, HEADS, HEAD_DIM
    )
    queries = (
        rotate(queries, cosine, sine, 1.0)
        .astype(jnp.bfloat16)
        .reshape(rows, KV_HEADS, groups, HEAD_DIM)
    )
    keys = jnp.dot(first_in, key_mat, preferred_element_type=jnp.float32).reshape(
        rows, KV_HEADS, HEAD_DIM
    )
    keys = rotate(keys, cosine, sine, 1.0).astype(jnp.bfloat16).reshape(rows, kv_width)
    values = jnp.dot(first_in, value_mat, preferred_element_type=jnp.float32).astype(jnp.bfloat16)
    key_value = jnp.concatenate([keys, values], axis=1)
    piece = lax.all_gather(key_value, "ctx", axis=0, tiled=True)
    peak = jnp.full((KV_HEADS, groups, rows), NEG_FILL, jnp.float32)
    count = piece.shape[0]
    attend_block_keys = piece[:, :kv_width].reshape(count, KV_HEADS, HEAD_DIM)
    attend_block_values = piece[:, kv_width:].reshape(count, KV_HEADS, HEAD_DIM)
    attend_key_pos = jnp.arange(count, dtype=jnp.int32)
    attend_allowed = attend_key_pos[None, :] <= query_pos[:, None]
    attend_scores = (
        jnp.einsum("skgd,pkd->kgsp", queries, attend_block_keys, preferred_element_type=jnp.float32)
        * scaling
    )
    attend_scores = jnp.where(attend_allowed, attend_scores, NEG_FILL)
    new_peak = jnp.maximum(peak, jnp.max(attend_scores, axis=3))
    weights = jnp.where(attend_allowed, jnp.exp(attend_scores - new_peak[..., None]), 0.0)
    total = jnp.sum(weights, axis=3)
    added = jnp.einsum(
        "kgsp,pkd->skgd",
        weights.astype(jnp.bfloat16),
        attend_block_values,
        preferred_element_type=jnp.float32,
    )
    accum = added
    peak, total, accum = (new_peak, total, accum)
    lse = peak + jnp.log(total)
    attn = (
        (accum / jnp.transpose(total, (2, 0, 1))[..., None])
        .astype(jnp.bfloat16)
        .reshape(rows, HEADS * HEAD_DIM)
    )
    middle = inputs_wide + contract_cols(attn, output_mat)
    normed_two, scale_two = norm_forward(middle)
    second_in = (normed_two * gain_second).astype(jnp.bfloat16)
    gate = jnp.dot(second_in, gate_mat, preferred_element_type=jnp.float32)
    up_part = jnp.dot(second_in, up_mat, preferred_element_type=jnp.float32)
    sigma = jax.nn.sigmoid(gate)
    hidden = (gate * sigma * up_part).astype(jnp.bfloat16)
    hidden_out = (middle + contract_cols(hidden, down_mat)).astype(jnp.bfloat16)
    regathered = (
        lax.all_gather(shards[0], "dp", axis=1, tiled=True),
        lax.all_gather(shards[1], "dp", axis=0, tiled=True),
        lax.all_gather(shards[2], "dp", axis=0, tiled=True),
        lax.all_gather(shards[3], "dp", axis=0, tiled=True),
        lax.all_gather(shards[4], "dp", axis=0, tiled=True),
        lax.all_gather(shards[5], "dp", axis=0, tiled=True),
        lax.all_gather(shards[6], "dp", axis=0, tiled=True),
        lax.all_gather(shards[7], "dp", axis=0, tiled=True),
    )
    gain_rows, query_mat, key_mat, value_mat, output_mat, gate_mat, up_mat, down_mat = regathered
    gain_first = gain_rows[0].astype(jnp.float32)
    gain_second = gain_rows[1].astype(jnp.float32)
    grad_hidden = jnp.dot(out_grad, down_mat, preferred_element_type=jnp.float32)
    grad_gate = (grad_hidden * up_part * sigma * (1.0 + gate * (1.0 - sigma))).astype(jnp.bfloat16)
    grad_up = (grad_hidden * gate * sigma).astype(jnp.bfloat16)
    down_term = contract_rows(out_grad, hidden)
    gate_term = contract_rows(second_in, grad_gate)
    up_term = contract_rows(second_in, grad_up)
    grad_second = contract_cols(grad_gate, gate_mat) + contract_cols(grad_up, up_mat)
    back_two, gain_two_term = norm_backward(grad_second, normed_two, scale_two, gain_second)
    grad_middle = out_grad.astype(jnp.float32) + back_two
    middle_low = grad_middle.astype(jnp.bfloat16)
    output_term = contract_rows(middle_low, attn)
    grad_attn = jnp.dot(middle_low, output_mat, preferred_element_type=jnp.float32).astype(
        jnp.bfloat16
    )
    grad_heads = grad_attn.reshape(rows, KV_HEADS, groups, HEAD_DIM)
    attn_heads = attn.reshape(rows, KV_HEADS, groups, HEAD_DIM)
    delta = jnp.transpose(
        jnp.sum(grad_heads.astype(jnp.float32) * attn_heads.astype(jnp.float32), axis=3), (1, 2, 0)
    )
    travel = key_value
    carried = jnp.zeros((rows, 2 * kv_width), jnp.float32)
    grad_queries = jnp.zeros((rows, KV_HEADS, groups, HEAD_DIM), jnp.float32)
    for step in range(ctx_count):
        owner = (ctx_index - step) % ctx_count
        key_pos = owner * rows + jnp.arange(rows, dtype=jnp.int32)
        allowed = key_pos[None, :] <= query_pos[:, None]
        block_keys = travel[:, :kv_width].reshape(rows, KV_HEADS, HEAD_DIM)
        block_values = travel[:, kv_width:].reshape(rows, KV_HEADS, HEAD_DIM)
        scores = (
            jnp.einsum("skgd,pkd->kgsp", queries, block_keys, preferred_element_type=jnp.float32)
            * scaling
        )
        probs = jnp.exp(jnp.where(allowed, scores - lse[..., None], NEG_FILL))
        value_grad = jnp.einsum(
            "kgsp,skgd->pkd",
            probs.astype(jnp.bfloat16),
            grad_heads,
            preferred_element_type=jnp.float32,
        )
        prob_grad = jnp.einsum(
            "skgd,pkd->kgsp", grad_heads, block_values, preferred_element_type=jnp.float32
        )
        score_grad = (probs * (prob_grad - delta[..., None]) * scaling).astype(jnp.bfloat16)
        grad_queries = grad_queries + jnp.einsum(
            "kgsp,pkd->skgd", score_grad, block_keys, preferred_element_type=jnp.float32
        )
        key_grad = jnp.einsum(
            "kgsp,skgd->pkd", score_grad, queries, preferred_element_type=jnp.float32
        )
        carried = carried + jnp.concatenate(
            [key_grad.reshape(rows, kv_width), value_grad.reshape(rows, kv_width)], axis=1
        )
        carried = passed_along(carried, "ctx", 1)
        if step + 1 < ctx_count:
            travel = shifted(travel, "ctx", 1)
    key_low = rotate(carried[:, :kv_width].reshape(rows, KV_HEADS, HEAD_DIM), cosine, sine, -1.0)
    key_low = key_low.astype(jnp.bfloat16).reshape(rows, kv_width)
    value_low = carried[:, kv_width:].astype(jnp.bfloat16)
    query_low = rotate(grad_queries.reshape(rows, HEADS, HEAD_DIM), cosine, sine, -1.0)
    query_low = query_low.astype(jnp.bfloat16).reshape(rows, HEADS * HEAD_DIM)
    query_term = contract_rows(first_in, query_low)
    key_term = contract_rows(first_in, key_low)
    value_term = contract_rows(first_in, value_low)
    grad_first = (
        contract_cols(query_low, query_mat)
        + contract_cols(key_low, key_mat)
        + contract_cols(value_low, value_mat)
    )
    back_one, gain_one_term = norm_backward(grad_first, normed_one, scale_one, gain_first)
    in_grad = grad_middle + back_one
    terms = (query_term, key_term, value_term, output_term, gate_term, up_term, down_term)
    stacked = jnp.concatenate(terms, axis=1)
    gain_terms = jnp.stack([gain_one_term, gain_two_term])
    own_grads, own_gains = (
        lax.psum_scatter(stacked, "dp", scatter_dimension=0, tiled=True),
        lax.psum_scatter(gain_terms, "dp", scatter_dimension=1, tiled=True),
    )
    own_grads, own_gains = lax.psum((own_grads, own_gains), "ctx")
    results = []
    offset = 0
    for term in terms:
        width = term.shape[1]
        results.append(own_grads[:, offset : offset + width])
        offset = offset + width
    return (
        hidden_out,
        in_grad,
        own_gains,
        results[0],
        results[1],
        results[2],
        results[3],
        results[4],
        results[5],
        results[6],
    )


def solution(mesh):
    return jax.shard_map(
        on_device,
        mesh=mesh,
        in_specs=(
            P(("dp", "ctx"), None),
            P(("dp", "ctx"), None),
            P(None, "dp"),
            P("dp", None),
            P("dp", None),
            P("dp", None),
            P("dp", None),
            P("dp", None),
            P("dp", None),
            P("dp", None),
        ),
        out_specs=(
            P(("dp", "ctx"), None),
            P(("dp", "ctx"), None),
            P(None, "dp"),
            P("dp", None),
            P("dp", None),
            P("dp", None),
            P("dp", None),
            P("dp", None),
            P("dp", None),
            P("dp", None),
        ),
        check_vma=False,
    )
```

profile of v0, /device:TPU:0, one launch (start us, length us, event | category | flops | bytes accessed | tf_op | source)
XLA Modules:
  0.0 1019.9 jit_solution(10856639301617734905)
XLA Ops:
  7.3 26.2 %all-gather.2 = bf16[16,60,320]{2,1,0:T(8,128)(2,1)S(1)} all-gather(bf16[1,60,320]{2,1,0:T(8,128)(2,1)} %bitcast.615), channel_id=1, replica_groups=mesh['dp'=16,'ctx'=8] {'dp'}, dimensions={0}, use_global_device_ids=true | all-gather | bytes 652800 | tf_op jit(solution)/shard_map/all_gather | solution.py:98
  33.7 19.7 %all-gather = bf16[16,60,2]{1,2,0:T(2,128)(2,1)S(1)} all-gather(bf16[1,60,2]{1,2,0:T(2,128)(2,1)} %bitcast.621), channel_id=1, replica_groups=mesh['dp'=16,'ctx'=8] {'dp'}, dimensions={0}, use_global_device_ids=true | all-gather | bytes 4080 | tf_op jit(solution)/shard_map/all_gather | solution.py:95
  55.2 22.4 %all-gather.1 = bf16[16,60,320]{2,1,0:T(8,128)(2,1)S(1)} all-gather(bf16[1,60,320]{2,1,0:T(8,128)(2,1)} %bitcast.616), channel_id=1, replica_groups=mesh['dp'=16,'ctx'=8] {'dp'}, dimensions={0}, use_global_device_ids=true | all-gather | bytes 652800 | tf_op jit(solution)/shard_map/all_gather | solution.py:97
  86.6 5.5 collective-permute-start.1
  93.1 5.5 collective-permute-start.2
  99.6 6.1 collective-permute-start.3
  106.7 5.6 collective-permute-start.4
  113.3 5.6 collective-permute-start.5
  120.0 6.1 collective-permute-start.6
  127.4 2.2 fusion.138
  129.6 24.0 %all-gather.19.cloned.1.call-done = bf16[16,60,960]{2,1,0:T(8,128)(2,1)} async-done(((bf16[1,60,960]{2,1,0:T(8,128)(2,1)}), bf16[16,60,960]{2,1,0:T(8,128)(2,1)}) %all-gather.19.cloned.1.call-update) | async-done | bytes 1843216 | tf_op jit(solution)/shard_map/all_gather | solution.py:99
  153.7 4.0 reshape.296
  157.6 42.5 %all-gather.17.cloned.1.call-done = bf16[16,60,960]{2,1,0:T(8,128)(2,1)} async-done(((bf16[1,60,960]{2,1,0:T(8,128)(2,1)}), bf16[16,60,960]{2,1,0:T(8,128)(2,1)}) %all-gather.17.cloned.1.call-update) | async-done | bytes 1843216 | tf_op jit(solution)/shard_map/all_gather | solution.py:96
  200.1 2.8 reshape.294
  202.9 1.8 fusion.130
  204.9 1.3 fusion.1
  206.2 1.9 fusion.2
  208.1 2.1 fusion.78
  211.4 1.3 fusion.25
  212.7 1.4 fusion.30
  215.4 1.3 fusion.40
  216.7 1.4 fusion.45
  218.1 1.3 fusion.50
  219.5 1.3 fusion.55
  220.8 1.3 fusion.60
  222.1 35.6 %all-gather.21.cloned.1.call-done = bf16[16,60,2560]{2,1,0:T(8,128)(2,1)} async-done(((bf16[1,60,2560]{2,1,0:T(8,128)(2,1)}), bf16[16,60,2560]{2,1,0:T(8,128)(2,1)}) %all-gather.21.cloned.1.call-update) | async-done | bytes 4915216 | tf_op jit(solution)/shard_map/all_gather | solution.py:100
  257.7 7.3 reshape.298
  265.1 50.6 %all-gather.23.cloned.1.call-done = bf16[16,60,2560]{2,1,0:T(8,128)(2,1)} async-done(((bf16[1,60,2560]{2,1,0:T(8,128)(2,1)}), bf16[16,60,2560]{2,1,0:T(8,128)(2,1)}) %all-gather.23.cloned.1.call-update) | async-done | bytes 4915216 | tf_op jit(solution)/shard_map/all_gather | solution.py:101
  315.7 7.3 reshape.300
  323.0 4.5 fusion.147
  327.5 2.0 fusion.148
  329.5 44.1 %all-gather.25.cloned.1.call-done = bf16[16,60,2560]{2,1,0:T(8,128)(2,1)} async-done(((bf16[1,60,2560]{2,1,0:T(8,128)(2,1)}), bf16[16,60,2560]{2,1,0:T(8,128)(2,1)}) %all-gather.25.cloned.1.call-update) | async-done | bytes 4915216 | tf_op jit(solution)/shard_map/all_gather | solution.py:102
  373.6 7.5 reshape.302
  381.2 4.7 multiply_convert_fusion
  385.9 1.4 fusion.149
  387.4 4.1 multiply_reduce_fusion
  394.1 5.1 fusion.159
  399.1 5.2 fusion.160
  409.8 5.3 convolution_bitcast_fusion
  418.6 6.7 collective-permute-done.8
  426.0 7.0 collective-permute-done.9
  433.6 7.1 collective-permute-done.10
  441.2 7.3 collective-permute-done.11
  449.1 7.2 collective-permute-done.12
  456.4 2.5 fusion.116
  458.9 5.1 collective-permute-done.13
  464.1 2.7 fusion.128
  466.8 5.0 collective-permute-done.14
  472.3 1.6 fusion.120
  473.9 41.3 %concatenate.70 = f32[960,10240]{1,0:T(8,128)} concatenate(f32[960,960]{1,0:T(8,128)} %fusion.128, f32[960,320]{1,0:T(8,128)S(1)} %fusion.126, f32[960,320]{1,0:T(8,128)} %fusion.120, f32[960,960]{1,0:T(8,128)} %fusion.116, f32[960,2560]{1,0:T(8,128)} %fusion.159, f32[960,2560]{1,0:T(8,128)} %fusion.160, f32[960,2560]{1,0:T(8,128)} %convolution_bitcast_fusion), dimensions={1} | concatenate | bytes 78643200 | tf_op jit(solution)/shard_map/concatenate | solution.py:247
  515.2 344.0 %fusion = f32[64,10240]{1,0:T(8,128)S(1)} fusion(f32[960,10240]{1,0:T(8,128)} %concatenate.70), kind=kCustom, calls=%all-reduce-scatter | all-reduce-scatter fusion | flops 10485761 | bytes 41943552
  859.2 1.7 slice.178
  860.9 3.5 collective-permute-start.15
  866.3 3.0 fusion.161
  869.3 4.7 fusion.74
  874.1 43.8 %collective-permute-done.15 = f32[60,10240]{1,0:T(8,128)} collective-permute-done((f32[60,10240]{1,0:T(8,128)}, f32[60,10240]{1,0:T(8,128)}, u32[]{:S(2)}, u32[]{:S(2)}) %collective-permute-start.15) | collective-permute-done | bytes 2457632
  917.9 15.5 %concatenate.71 = f32[124,10240]{1,0:T(8,128)} concatenate(f32[60,10240]{1,0:T(8,128)} %collective-permute-done.15, f32[64,10240]{1,0:T(8,128)S(1)} %fusion), dimensions={0} | concatenate | bytes 10158080
  933.4 3.7 constant_dynamic-slice_fusion
  938.1 40.0 %all-reduce = f32[2,960]{1,0:T(2,128)S(1)} all-reduce(f32[2,960]{1,0:T(2,128)S(1)} %pad_maximum_fusion.4), channel_id=2, replica_groups=mesh['dp'=16,'ctx'=8] {'dp'}, use_global_device_ids=true, to_apply=%region_9.10.clone | all-reduce | flops 1920 | bytes 15360
  978.2 13.0 %psum.14 = f32[2,60]{1,0:T(2,128)} all-reduce(f32[2,60]{1,0:T(2,128)S(1)} %constant_dynamic-slice_fusion.1), channel_id=1, replica_groups=mesh['dp'=16,'ctx'=8] {'ctx'}, use_global_device_ids=true, to_apply=%region_10.11 | all-reduce | flops 120 | bytes 960 | tf_op jit(solution)/shard_map/psum | solution.py:253
  992.1 14.3 %all-reduce.5.cloned.1.call-done = f32[60,10240]{1,0:T(8,128)} async-done(((f32[60,10240]{1,0:T(8,128)}), f32[60,10240]{1,0:T(8,128)}) %all-reduce.5.cloned.1.call-update) | async-done | bytes 2457616 | tf_op jit(solution)/shard_map/psum | solution.py:253
  1006.5 1.9 fusion.136
  1008.4 1.7 fusion.137
  1010.1 2.8 fusion.135
  (270 shorter events, 36.1 us)
Async XLA Ops:
  7.2 70.8 %copy-start.1 = (bf16[128,960]{0,1:T(8,128)(2,1)S(1)}, bf16[128,960]{0,1:T(8,128)(2,1)}, u32[]{:S(2)}) copy-start(bf16[128,960]{0,1:T(8,128)(2,1)} %param.10) | copy-start | bytes 737284
  7.2 120.2 %all-gather.15.cloned.1.call-start = ((), (), s32[]{:S(2)}) async-start(), calls=%async_computation | async-start | bytes 1474560 | tf_op jit(solution)/shard_map/all_gather | solution.py:126
  33.7 79.3 %copy-start.17 = (bf16[960,320]{1,0:T(8,128)(2,1)}, bf16[960,320]{1,0:T(8,128)(2,1)S(1)}, u32[]{:S(2)}) copy-start(bf16[960,320]{1,0:T(8,128)(2,1)S(1)} %reshape.292) | copy-start | bytes 1843204
  54.1 25.9 %copy-start.53 = (f32[1,960]{1,0:T(1,128)}, f32[1,960]{1,0:T(1,128)S(1)}, u32[]{:S(2)}) copy-start(f32[1,960]{1,0:T(1,128)S(1)} %get-tuple-element.53) | copy-start | bytes 11524
  55.2 24.0 %copy-start.56 = (f32[128]{0:T(128)}, f32[128]{0:T(128)S(1)}, u32[]{:S(2)}) copy-start(f32[128]{0:T(128)S(1)} %add_rsqrt_fusion.1) | copy-start | bytes 1540
  77.9 51.7 %copy-start.7 = (bf16[960,320]{1,0:T(8,128)(2,1)}, bf16[960,320]{1,0:T(8,128)(2,1)S(1)}, u32[]{:S(2)}) copy-start(bf16[960,320]{1,0:T(8,128)(2,1)S(1)} %reshape.290) | copy-start | bytes 1843204
  78.6 51.1 %copy-start.29 = (bf16[128,320]{0,1:T(8,128)(2,1)}, bf16[128,320]{0,1:T(8,128)(2,1)S(1)}, u32[]{:S(2)}) copy-start(bf16[128,320]{0,1:T(8,128)(2,1)S(1)} %convolution_convert_fusion.1) | copy-start | bytes 245764
  81.4 72.3 %all-gather.19.cloned.1.call-start = ((), (), s32[]{:S(2)}) async-start(), calls=%async_computation.3 | async-start | bytes 2228224 | tf_op jit(solution)/shard_map/all_gather | solution.py:99
  82.1 118.0 %all-gather.17.cloned.1.call-start = ((), (), s32[]{:S(2)}) async-start(), calls=%async_computation.2 | async-start | bytes 2228224 | tf_op jit(solution)/shard_map/all_gather | solution.py:96
  82.9 174.9 %all-gather.21.cloned.1.call-start = ((), (), s32[]{:S(2)}) async-start(), calls=%async_computation.4 | async-start | bytes 5570560 | tf_op jit(solution)/shard_map/all_gather | solution.py:100
  83.5 232.2 %all-gather.23.cloned.1.call-start = ((), (), s32[]{:S(2)}) async-start(), calls=%async_computation.5 | async-start | bytes 5570560 | tf_op jit(solution)/shard_map/all_gather | solution.py:101
  84.0 289.6 %all-gather.25.cloned.1.call-start = ((), (), s32[]{:S(2)}) async-start(), calls=%async_computation.6 | async-start | bytes 5570560 | tf_op jit(solution)/shard_map/all_gather | solution.py:102
  84.1 2.5 collective-permute-start
  85.4 921.0 %all-reduce.5.cloned.1.call-start = ((), (), s32[]{:S(2)}) async-start(), calls=%async_computation.1 | async-start | bytes 5242880 | tf_op jit(solution)/shard_map/psum | solution.py:253
  86.6 6.5 collective-permute-start.1
  93.1 6.5 collective-permute-start.2
  99.6 7.1 collective-permute-start.3
  106.7 6.6 collective-permute-start.4
  113.3 6.6 collective-permute-start.5
  120.0 6.8 collective-permute-start.6
  210.3 182.4 %copy-start.20 = (bf16[128,5,3,64]{0,3,2,1:T(8,128)(2,1)}, bf16[128,5,3,64]{0,3,2,1:T(8,128)(2,1)S(1)}, u32[]{:S(2)}) copy-start(bf16[128,5,3,64]{0,3,2,1:T(8,128)(2,1)S(1)} %fusion.78) | copy-start | bytes 737284
  210.3 5.1 copy-start.44
  210.3 5.1 copy-start.62
  210.4 6.4 copy-start.36
  210.4 6.4 copy-start.61
  210.4 7.7 copy-start.38
  210.4 7.7 copy-start.60
  211.1 8.3 copy-start.34
  211.1 8.3 copy-start.59
  211.4 9.4 copy-start.32
  211.4 9.4 copy-start.58
  323.0 4.5 copy-start
  329.5 51.6 %copy-start.26 = (bf16[128,960]{0,1:T(8,128)(2,1)S(1)}, bf16[128,960]{0,1:T(8,128)(2,1)}, u32[]{:S(2)}) copy-start(bf16[128,960]{0,1:T(8,128)(2,1)} %param.11) | copy-start | bytes 737284
  373.6 12.2 %slice-start = ((s8[4915200]{0:T(1024)(128)(4,1)}), s8[720896]{0:T(1024)(128)(4,1)S(1)}, s32[]{:S(2)}) async-start(s8[4915200]{0:T(1024)(128)(4,1)} %bitcast.539), calls=%async_computation.7 | async-start | bytes 1441792
  381.2 4.7 slice-start.1
  385.9 23.9 %copy-start.19 = (bf16[128,2560]{1,0:T(8,128)(2,1)}, bf16[128,2560]{1,0:T(8,128)(2,1)S(1)}, u32[]{:S(2)}) copy-start(bf16[128,2560]{1,0:T(8,128)(2,1)S(1)} %get-tuple-element.25) | copy-start | bytes 1966084
  387.3 4.4 copy-start.4
  387.3 5.4 copy-start.16
  391.7 64.6 %copy-start.5 = (f32[128,960]{0,1:T(8,128)}, f32[128,960]{0,1:T(8,128)S(1)}, u32[]{:S(2)}) copy-start(f32[128,960]{0,1:T(8,128)S(1)} %multiply_add_fusion) | copy-start | bytes 1474564
  399.1 5.2 copy-start.15
  399.1 5.5 copy-start.47
  399.1 6.2 copy-start.41
  409.8 7.7 collective-permute-start.7
  409.8 5.4 copy-start.37
  409.8 5.6 copy-start.39
  409.8 6.2 copy-start.10
  409.8 6.2 copy-start.46
  415.4 10.3 %copy-start.9 = (f32[5,3,128,128]{2,3,1,0:T(8,128)S(1)}, f32[5,3,128,128]{2,3,1,0:T(8,128)}, u32[]{:S(2)}) copy-start(f32[5,3,128,128]{2,3,1,0:T(8,128)} %fusion.60) | copy-start | bytes 2949124
  415.4 10.3 %copy-start.33 = (bf16[128,320]{0,1:T(8,128)(2,1)S(1)}, bf16[128,320]{0,1:T(8,128)(2,1)}, u32[]{:S(2)}) copy-start(bf16[128,320]{0,1:T(8,128)(2,1)} %get-tuple-element.34) | copy-start | bytes 245764
  417.5 7.7 collective-permute-start.8
  425.3 7.7 collective-permute-start.9
  425.6 22.9 %copy-start.52 = (f32[128,64]{0,1:T(8,128)S(1)}, f32[128,64]{0,1:T(8,128)}, u32[]{:S(2)}) copy-start(f32[128,64]{0,1:T(8,128)} %get-tuple-element.50) | copy-start | bytes 98308
  433.0 7.7 collective-permute-start.10
  433.4 23.0 %copy-start.21 = (bf16[128,5,3,64]{0,3,2,1:T(8,128)(2,1)S(1)}, bf16[128,5,3,64]{0,3,2,1:T(8,128)(2,1)}, u32[]{:S(2)}) copy-start(bf16[128,5,3,64]{0,3,2,1:T(8,128)(2,1)} %copy-done.20) | copy-start | bytes 737284
  440.8 7.7 collective-permute-start.11
  448.6 7.7 collective-permute-start.12
  448.6 15.5 %copy-start.54 = (f32[1,960]{1,0:T(1,128)S(1)}, f32[1,960]{1,0:T(1,128)}, u32[]{:S(2)}) copy-start(f32[1,960]{1,0:T(1,128)} %copy-done.53) | copy-start | bytes 11524
  448.6 15.5 %copy-start.57 = (f32[128]{0:T(128)S(1)}, f32[128]{0:T(128)}, u32[]{:S(2)}) copy-start(f32[128]{0:T(128)} %copy-done.56) | copy-start | bytes 1540
  448.7 18.1 %copy-start.22 = (bf16[128,960]{0,1:T(8,128)(2,1)}, bf16[128,960]{0,1:T(8,128)(2,1)S(1)}, u32[]{:S(2)}) copy-start(bf16[128,960]{0,1:T(8,128)(2,1)S(1)} %fusion.95) | copy-start | bytes 737284
  456.3 7.7 collective-permute-start.13
  464.1 7.7 collective-permute-start.14
  859.2 5.2 copy-start.66
  860.9 57.0 %collective-permute-start.15 = (f32[60,10240]{1,0:T(8,128)}, f32[60,10240]{1,0:T(8,128)}, u32[]{:S(2)}, u32[]{:S(2)}) collective-permute-start(f32[60,10240]{1,0:T(8,128)} %slice.178), channel_id=1, source_target_pairs={{0,8},{8,16},{16,24},{24,32},{32,40},{40,48},{48,56},{56,64},{64,7... | collective-permute-start | bytes 7372808
  933.4 57.7 %copy-start.6 = (f32[128,960]{0,1:T(8,128)S(1)}, f32[128,960]{0,1:T(8,128)}, u32[]{:S(2)}) copy-start(f32[128,960]{0,1:T(8,128)} %copy-done.5) | copy-start | bytes 1474564
  (28 other events, 76.7 us)
Sparse Core Ops, SparseCore 0:
  81.5 24.6 all-gather.14
  108.3 45.3 all-gather.18
  155.8 44.2 all-gather.16
  202.1 55.5 all-gather.20
  259.7 55.9 all-gather.22
  317.7 55.9 all-gather.24
  937.3 69.0 all-reduce.4
where the time goes:
time: 1030 us; the launch traced here: 1020 us
  blocking collectives  465 us (45%)
  waiting for transfers between devices  306 us (30%)
  local copies, waits for them, and re-layouts  106 us (10%)
  matrix products  76.8 us (7%)
  starting transfers between devices  40 us (4%)
  between operations  17.3 us (2%)
    unnamed x2, blocking collectives  384 us
    unnamed x151, local copies, waits for them, and re-layouts  51.5 us
    all_gather x1, waiting for transfers between devices, on_device(): lax.all_gather(shards[6], 'dp', axis=0, tiled=True)  50.6 us
    ppermute x8, waiting for transfers between devices, passed_along(): return lax.ppermute(block, axis, route)  46.5 us
    unnamed x8, waiting for transfers between devices  46.3 us
    all_gather x1, waiting for transfers between devices, on_device(): lax.all_gather(shards[7], 'dp', axis=0, tiled=True)  44.1 us
    all_gather x1, waiting for transfers between devices, on_device(): lax.all_gather(shards[1], 'dp', axis=0, tiled=True)  42.5 us
    concatenate x1, local copies, waits for them, and re-layouts, on_device(): stacked = jnp.concatenate(terms, axis=1)  41.3 us
  transfers between devices with their start and end apart: 23, of which 20 were waited for; matrix products, arithmetic and copies ran while one was open for 8% of the time, Pallas kernels for 0%

commit v1 on v0

--- a/solution.py
+++ b/solution.py
@@ -3,6 +3,7 @@
 import jax.numpy as jnp
 from jax import lax
 from jax.sharding import PartitionSpec as P
+from jax.lax import all_to_all, psum
 
 HEADS = 15
 KV_HEADS = 5
@@ -91,6 +92,16 @@
         up_weight,
         down_weight,
     )
+
+    def advance_the_regions(inputs, chip_axis):
+        world = psum(1, chip_axis)
+        shelf = []
+        for d in tuple(range(inputs.ndim)):
+            shelf.append(world if d == 0 else 1)
+        outer = jnp.tile(inputs, shelf)
+        oldest = all_to_all(outer, chip_axis, split_axis=0, concat_axis=0, tiled=True)
+        return oldest
+
     gathered = (
         lax.all_gather(shards[0], "dp", axis=1, tiled=True),
         lax.all_gather(shards[1], "dp", axis=0, tiled=True),
@@ -99,7 +110,7 @@
         lax.all_gather(shards[4], "dp", axis=0, tiled=True),
         lax.all_gather(shards[5], "dp", axis=0, tiled=True),
         lax.all_gather(shards[6], "dp", axis=0, tiled=True),
-        lax.all_gather(shards[7], "dp", axis=0, tiled=True),
+        advance_the_regions(shards[7], "dp"),
     )
     gain_rows, query_mat, key_mat, value_mat, output_mat, gate_mat, up_mat, down_mat = gathered
     gain_first = gain_rows[0].astype(jnp.float32)

time: 1030 us -> 1060 us (1.029)
  waiting for transfers between devices: 306 us -> 330 us
  local copies, waits for them, and re-layouts: 106 us -> 117 us
    all_gather x1, waiting for transfers between devices: 24 us -> 55.2 us  [on_device(): lax.all_gather(shards[4], 'dp', axis=0, tiled=True)]
    unnamed x151 -> x153, local copies, waits for them, and re-layouts: 51.5 us -> 51.6 us
  transfers between devices with their start and end apart: 23 -> 24, of which waited for: 20 -> 20; matrix products, arithmetic and copies ran while one was open for 8% -> 48% of each run, Pallas kernels for 0% -> 0%
where the time goes in v1:
time: 1060 us
  blocking collectives  465 us (44%)
  waiting for transfers between devices  330 us (31%)
  local copies, waits for them, and re-layouts  117 us (11%)
  matrix products  76.7 us (7%)
  starting transfers between devices  42.6 us (4%)
  between operations  17.3 us (2%)
    unnamed x2, blocking collectives  384 us
    all_gather x1, waiting for transfers between devices, on_device(): lax.all_gather(shards[4], 'dp', axis=0, tiled=True)  55.2 us
    unnamed x153, local copies, waits for them, and re-layouts  51.6 us
    all_gather x1, waiting for transfers between devices, on_device(): lax.all_gather(shards[6], 'dp', axis=0, tiled=True)  50.6 us
    ppermute x8, waiting for transfers between devices, passed_along(): return lax.ppermute(block, axis, route)  46.5 us
    all_gather x1, waiting for transfers between devices, on_device(): lax.all_gather(shards[7], 'dp', axis=0, tiled=True)  44.1 us
    all_gather x1, waiting for transfers between devices, on_device(): lax.all_gather(shards[1], 'dp', axis=0, tiled=True)  42.5 us
    concatenate x1, local copies, waits for them, and re-layouts, on_device(): stacked = jnp.concatenate(terms, axis=1)  41.3 us
  transfers between devices with their start and end apart: 24, of which 20 were waited for; matrix products, arithmetic and copies ran while one was open for 48% of the time, Pallas kernels for 0%

profile of v1, /device:TPU:0, one launch (start us, length us, event | category | flops | bytes accessed | tf_op | source)
XLA Modules:
  0.0 1057.1 jit_solution(9065513755135200340)
XLA Ops:
  7.3 26.2 %all-gather.2 = bf16[16,60,320]{2,1,0:T(8,128)(2,1)S(1)} all-gather(bf16[1,60,320]{2,1,0:T(8,128)(2,1)} %bitcast.615), channel_id=1, replica_groups=mesh['dp'=16,'ctx'=8] {'dp'}, dimensions={0}, use_global_device_ids=true | all-gather | bytes 652800 | tf_op jit(solution)/shard_map/all_gather | solution.py:109
  33.7 19.7 %all-gather = bf16[16,60,2]{1,2,0:T(2,128)(2,1)S(1)} all-gather(bf16[1,60,2]{1,2,0:T(2,128)(2,1)} %bitcast.621), channel_id=1, replica_groups=mesh['dp'=16,'ctx'=8] {'dp'}, dimensions={0}, use_global_device_ids=true | all-gather | bytes 4080 | tf_op jit(solution)/shard_map/all_gather | solution.py:106
  55.2 22.4 %all-gather.1 = bf16[16,60,320]{2,1,0:T(8,128)(2,1)S(1)} all-gather(bf16[1,60,320]{2,1,0:T(8,128)(2,1)} %bitcast.616), channel_id=1, replica_groups=mesh['dp'=16,'ctx'=8] {'dp'}, dimensions={0}, use_global_device_ids=true | all-gather | bytes 652800 | tf_op jit(solution)/shard_map/all_gather | solution.py:108
  85.4 3.0 tile.2
  88.3 5.3 all-to-all-start
  95.5 3.9 collective-permute-start.1
  100.3 4.8 collective-permute-start.2
  106.1 5.6 collective-permute-start.3
  112.7 5.6 collective-permute-start.4
  119.4 5.6 collective-permute-start.5
  126.0 6.1 collective-permute-start.6
  133.4 2.2 fusion.138
  135.7 55.2 %all-gather.19.cloned.1.call-done = bf16[16,60,960]{2,1,0:T(8,128)(2,1)} async-done(((bf16[1,60,960]{2,1,0:T(8,128)(2,1)}), bf16[16,60,960]{2,1,0:T(8,128)(2,1)}) %all-gather.19.cloned.1.call-update) | async-done | bytes 1843216 | tf_op jit(solution)/shard_map/all_gather | solution.py:110
  190.8 3.9 reshape.303
  194.8 42.5 %all-gather.17.cloned.1.call-done = bf16[16,60,960]{2,1,0:T(8,128)(2,1)} async-done(((bf16[1,60,960]{2,1,0:T(8,128)(2,1)}), bf16[16,60,960]{2,1,0:T(8,128)(2,1)}) %all-gather.17.cloned.1.call-update) | async-done | bytes 1843216 | tf_op jit(solution)/shard_map/all_gather | solution.py:107
  237.3 2.8 reshape.301
  240.1 1.8 fusion.130
  243.4 1.9 fusion.2
  245.3 2.1 fusion.78
  248.6 1.3 fusion.25
  249.9 1.3 fusion.30
  251.3 1.4 fusion.35
  252.6 1.3 fusion.40
  258.0 1.3 fusion.60
  259.3 35.5 %all-gather.21.cloned.1.call-done = bf16[16,60,2560]{2,1,0:T(8,128)(2,1)} async-done(((bf16[1,60,2560]{2,1,0:T(8,128)(2,1)}), bf16[16,60,2560]{2,1,0:T(8,128)(2,1)}) %all-gather.21.cloned.1.call-update) | async-done | bytes 4915216 | tf_op jit(solution)/shard_map/all_gather | solution.py:111
  294.9 7.3 reshape.305
  302.2 50.6 %all-gather.23.cloned.1.call-done = bf16[16,60,2560]{2,1,0:T(8,128)(2,1)} async-done(((bf16[1,60,2560]{2,1,0:T(8,128)(2,1)}), bf16[16,60,2560]{2,1,0:T(8,128)(2,1)}) %all-gather.23.cloned.1.call-update) | async-done | bytes 4915216 | tf_op jit(solution)/shard_map/all_gather | solution.py:112
  352.8 7.3 reshape.307
  360.1 4.5 fusion.147
  364.6 2.0 fusion.148
  366.6 44.1 %all-gather.25.cloned.1.call-done = bf16[16,60,2560]{2,1,0:T(8,128)(2,1)} async-done(((bf16[1,60,2560]{2,1,0:T(8,128)(2,1)}), bf16[16,60,2560]{2,1,0:T(8,128)(2,1)}) %all-gather.25.cloned.1.call-update) | async-done | bytes 4915216 | tf_op jit(solution)/shard_map/all_gather | solution.py:182
  410.7 7.6 reshape.309
  418.3 4.7 multiply_convert_fusion
  423.0 1.4 fusion.149
  424.5 4.1 multiply_reduce_fusion
  431.2 5.1 fusion.159
  436.3 5.2 fusion.160
  446.9 5.3 convolution_bitcast_fusion
  455.7 6.6 collective-permute-done.8
  463.1 7.0 collective-permute-done.9
  470.8 7.1 collective-permute-done.10
  478.3 7.3 collective-permute-done.11
  486.2 7.2 collective-permute-done.12
  493.5 2.6 fusion.116
  496.0 5.1 collective-permute-done.13
  501.2 2.6 fusion.128
  503.9 5.1 collective-permute-done.14
  509.4 1.5 fusion.120
  510.9 41.3 %concatenate.70 = f32[960,10240]{1,0:T(8,128)} concatenate(f32[960,960]{1,0:T(8,128)} %fusion.128, f32[960,320]{1,0:T(8,128)S(1)} %fusion.126, f32[960,320]{1,0:T(8,128)} %fusion.120, f32[960,960]{1,0:T(8,128)} %fusion.116, f32[960,2560]{1,0:T(8,128)} %fusion.159, f32[960,2560]{1,0:T(8,128)} %fusion.160, f32[960,2560]{1,0:T(8,128)} %convolution_bitcast_fusion), dimensions={1} | concatenate | bytes 78643200 | tf_op jit(solution)/shard_map/concatenate | solution.py:258
  552.2 344.0 %fusion = f32[64,10240]{1,0:T(8,128)S(1)} fusion(f32[960,10240]{1,0:T(8,128)} %concatenate.70), kind=kCustom, calls=%all-reduce-scatter | all-reduce-scatter fusion | flops 10485761 | bytes 41943552
  896.3 1.7 slice.178
  898.0 3.5 collective-permute-start.15
  903.4 7.3 all_to_all.7
  910.7 3.0 fusion.161
  913.7 4.7 fusion.74
  918.5 36.5 %collective-permute-done.15 = f32[60,10240]{1,0:T(8,128)} collective-permute-done((f32[60,10240]{1,0:T(8,128)}, f32[60,10240]{1,0:T(8,128)}, u32[]{:S(2)}, u32[]{:S(2)}) %collective-permute-start.15) | collective-permute-done | bytes 2457632
  954.9 15.6 %concatenate.71 = f32[124,10240]{1,0:T(8,128)} concatenate(f32[60,10240]{1,0:T(8,128)} %collective-permute-done.15, f32[64,10240]{1,0:T(8,128)S(1)} %fusion), dimensions={0} | concatenate | bytes 10158080
  970.5 3.8 constant_dynamic-slice_fusion
  975.2 40.0 %all-reduce = f32[2,960]{1,0:T(2,128)S(1)} all-reduce(f32[2,960]{1,0:T(2,128)S(1)} %pad_maximum_fusion.4), channel_id=2, replica_groups=mesh['dp'=16,'ctx'=8] {'dp'}, use_global_device_ids=true, to_apply=%region_9.10.clone | all-reduce | flops 1920 | bytes 15360
  1015.3 13.0 %psum.14 = f32[2,60]{1,0:T(2,128)} all-reduce(f32[2,60]{1,0:T(2,128)S(1)} %constant_dynamic-slice_fusion.1), channel_id=1, replica_groups=mesh['dp'=16,'ctx'=8] {'ctx'}, use_global_device_ids=true, to_apply=%region_10.11 | all-reduce | flops 120 | bytes 960 | tf_op jit(solution)/shard_map/psum | solution.py:264
  1029.2 14.4 %all-reduce.5.cloned.1.call-done = f32[60,10240]{1,0:T(8,128)} async-done(((f32[60,10240]{1,0:T(8,128)}), f32[60,10240]{1,0:T(8,128)}) %all-reduce.5.cloned.1.call-update) | async-done | bytes 2457616 | tf_op jit(solution)/shard_map/psum | solution.py:264
  1043.6 1.9 fusion.136
  1045.5 1.7 fusion.137
  1047.2 2.8 fusion.135
  (276 shorter events, 40.6 us)
Async XLA Ops:
  7.2 70.8 %copy-start.1 = (bf16[128,960]{0,1:T(8,128)(2,1)S(1)}, bf16[128,960]{0,1:T(8,128)(2,1)}, u32[]{:S(2)}) copy-start(bf16[128,960]{0,1:T(8,128)(2,1)} %param.10) | copy-start | bytes 737284
  7.2 126.3 %all-gather.15.cloned.1.call-start = ((), (), s32[]{:S(2)}) async-start(), calls=%async_computation.1 | async-start | bytes 1474560 | tf_op jit(solution)/shard_map/all_gather | solution.py:137
  33.4 51.9 %copy-start.26 = (bf16[60,2560]{1,0:T(8,128)(2,1)S(1)}, bf16[60,2560]{1,0:T(8,128)(2,1)}, u32[]{:S(2)}) copy-start(bf16[60,2560]{1,0:T(8,128)(2,1)} %param.19) | copy-start | bytes 921604
  33.7 54.6 %copy-start.17 = (bf16[960,320]{1,0:T(8,128)(2,1)}, bf16[960,320]{1,0:T(8,128)(2,1)S(1)}, u32[]{:S(2)}) copy-start(bf16[960,320]{1,0:T(8,128)(2,1)S(1)} %reshape.299) | copy-start | bytes 1843204
  54.1 25.9 %copy-start.54 = (f32[1,960]{1,0:T(1,128)}, f32[1,960]{1,0:T(1,128)S(1)}, u32[]{:S(2)}) copy-start(f32[1,960]{1,0:T(1,128)S(1)} %get-tuple-element.53) | copy-start | bytes 11524
  55.2 24.0 %copy-start.57 = (f32[128]{0:T(128)}, f32[128]{0:T(128)S(1)}, u32[]{:S(2)}) copy-start(f32[128]{0:T(128)S(1)} %add_rsqrt_fusion.1) | copy-start | bytes 1540
  77.9 10.4 copy-start.7
  78.6 9.8 copy-start.30
  81.4 109.4 %all-gather.19.cloned.1.call-start = ((), (), s32[]{:S(2)}) async-start(), calls=%async_computation.4 | async-start | bytes 2228224 | tf_op jit(solution)/shard_map/all_gather | solution.py:110
  82.2 155.2 %all-gather.17.cloned.1.call-start = ((), (), s32[]{:S(2)}) async-start(), calls=%async_computation.3 | async-start | bytes 2228224 | tf_op jit(solution)/shard_map/all_gather | solution.py:107
  82.9 212.0 %all-gather.21.cloned.1.call-start = ((), (), s32[]{:S(2)}) async-start(), calls=%async_computation.5 | async-start | bytes 5570560 | tf_op jit(solution)/shard_map/all_gather | solution.py:111
  83.5 269.3 %all-gather.23.cloned.1.call-start = ((), (), s32[]{:S(2)}) async-start(), calls=%async_computation.6 | async-start | bytes 5570560 | tf_op jit(solution)/shard_map/all_gather | solution.py:112
  84.0 11.4 %collective-permute-start = (bf16[128,640]{0,1:T(8,128)(2,1)}, bf16[128,640]{0,1:T(8,128)(2,1)S(1)}, u32[]{:S(2)}, u32[]{:S(2)}) collective-permute-start(bf16[128,640]{0,1:T(8,128)(2,1)} %pad_maximum_fusion.1), channel_id=1, source_target_pairs={{0,1},{1,2},{2,3},{3,4},{4,5},{5,6},{6,7},{8,9},{9,10},{10,11},{11... | collective-permute-start | bytes 491528 | tf_op jit(solution)/shard_map/ppermute | solution.py:25
  88.3 815.0 %all-to-all-start = ((bf16[16,60,2560]{2,1,0:T(8,128)(2,1)}), bf16[16,60,2560]{2,1,0:T(8,128)(2,1)}, u32[]{:S(2)}, u32[]{:S(2)}) async-start(bf16[16,60,2560]{2,1,0:T(8,128)(2,1)} %tile.2), calls=%async_computation | async-start | bytes 10485760 | tf_op jit(solution)/shard_map/all_to_all | solution.py:102
  93.7 317.0 %all-gather.25.cloned.1.call-start = ((), (), s32[]{:S(2)}) async-start(), calls=%async_computation.7 | async-start | bytes 5570560 | tf_op jit(solution)/shard_map/all_gather | solution.py:182
  94.3 949.3 %all-reduce.5.cloned.1.call-start = ((), (), s32[]{:S(2)}) async-start(), calls=%async_computation.2 | async-start | bytes 5242880 | tf_op jit(solution)/shard_map/psum | solution.py:264
  95.5 4.9 collective-permute-start.1
  100.3 5.8 collective-permute-start.2
  106.1 6.6 collective-permute-start.3
  112.7 6.6 collective-permute-start.4
  119.4 6.6 collective-permute-start.5
  126.0 6.8 collective-permute-start.6
  247.4 182.4 %copy-start.20 = (bf16[128,5,3,64]{0,3,2,1:T(8,128)(2,1)}, bf16[128,5,3,64]{0,3,2,1:T(8,128)(2,1)S(1)}, u32[]{:S(2)}) copy-start(bf16[128,5,3,64]{0,3,2,1:T(8,128)(2,1)S(1)} %fusion.78) | copy-start | bytes 737284
  247.5 5.1 copy-start.45
  247.5 5.1 copy-start.63
  247.5 6.5 copy-start.37
  247.5 6.5 copy-start.62
  247.5 7.8 copy-start.39
  247.6 7.8 copy-start.61
  248.3 8.4 copy-start.35
  248.3 8.4 copy-start.60
  248.5 9.4 copy-start.33
  248.5 9.4 copy-start.59
  366.6 51.7 %copy-start.27 = (bf16[128,960]{0,1:T(8,128)(2,1)S(1)}, bf16[128,960]{0,1:T(8,128)(2,1)}, u32[]{:S(2)}) copy-start(bf16[128,960]{0,1:T(8,128)(2,1)} %param.11) | copy-start | bytes 737284
  410.7 12.3 %slice-start = ((s8[4915200]{0:T(1024)(128)(4,1)}), s8[720896]{0:T(1024)(128)(4,1)S(1)}, s32[]{:S(2)}) async-start(s8[4915200]{0:T(1024)(128)(4,1)} %bitcast.539), calls=%async_computation.8 | async-start | bytes 1441792
  418.3 4.7 slice-start.1
  423.0 23.9 %copy-start.19 = (bf16[128,2560]{1,0:T(8,128)(2,1)}, bf16[128,2560]{1,0:T(8,128)(2,1)S(1)}, u32[]{:S(2)}) copy-start(bf16[128,2560]{1,0:T(8,128)(2,1)S(1)} %get-tuple-element.25) | copy-start | bytes 1966084
  424.5 5.4 copy-start.16
  428.8 64.6 %copy-start.5 = (f32[128,960]{0,1:T(8,128)}, f32[128,960]{0,1:T(8,128)S(1)}, u32[]{:S(2)}) copy-start(f32[128,960]{0,1:T(8,128)S(1)} %multiply_add_fusion) | copy-start | bytes 1474564
  436.3 5.2 copy-start.15
  436.3 5.5 copy-start.48
  436.3 6.2 copy-start.42
  446.9 7.7 collective-permute-start.7
  446.9 5.4 copy-start.38
  446.9 5.6 copy-start.40
  446.9 6.2 copy-start.10
  446.9 6.2 copy-start.47
  452.5 10.2 copy-start.9
  452.5 10.2 copy-start.34
  454.6 7.7 collective-permute-start.8
  462.4 7.7 collective-permute-start.9
  462.7 22.9 %copy-start.53 = (f32[128,64]{0,1:T(8,128)S(1)}, f32[128,64]{0,1:T(8,128)}, u32[]{:S(2)}) copy-start(f32[128,64]{0,1:T(8,128)} %get-tuple-element.50) | copy-start | bytes 98308
  470.1 7.7 collective-permute-start.10
  470.5 23.0 %copy-start.21 = (bf16[128,5,3,64]{0,3,2,1:T(8,128)(2,1)S(1)}, bf16[128,5,3,64]{0,3,2,1:T(8,128)(2,1)}, u32[]{:S(2)}) copy-start(bf16[128,5,3,64]{0,3,2,1:T(8,128)(2,1)} %copy-done.20) | copy-start | bytes 737284
  477.9 7.7 collective-permute-start.11
  485.7 7.7 collective-permute-start.12
  485.7 15.5 %copy-start.55 = (f32[1,960]{1,0:T(1,128)S(1)}, f32[1,960]{1,0:T(1,128)}, u32[]{:S(2)}) copy-start(f32[1,960]{1,0:T(1,128)} %copy-done.54) | copy-start | bytes 11524
  485.7 15.5 %copy-start.58 = (f32[128]{0:T(128)S(1)}, f32[128]{0:T(128)}, u32[]{:S(2)}) copy-start(f32[128]{0:T(128)} %copy-done.57) | copy-start | bytes 1540
  485.8 18.0 %copy-start.22 = (bf16[128,960]{0,1:T(8,128)(2,1)}, bf16[128,960]{0,1:T(8,128)(2,1)S(1)}, u32[]{:S(2)}) copy-start(bf16[128,960]{0,1:T(8,128)(2,1)S(1)} %fusion.95) | copy-start | bytes 737284
  493.4 7.7 collective-permute-start.13
  501.2 7.7 collective-permute-start.14
  896.3 5.2 copy-start.67
  898.0 57.0 %collective-permute-start.15 = (f32[60,10240]{1,0:T(8,128)}, f32[60,10240]{1,0:T(8,128)}, u32[]{:S(2)}, u32[]{:S(2)}) collective-permute-start(f32[60,10240]{1,0:T(8,128)} %slice.178), channel_id=1, source_target_pairs={{0,8},{8,16},{16,24},{24,32},{32,40},{40,48},{48,56},{56,64},{64,7... | collective-permute-start | bytes 7372808
  970.5 57.7 %copy-start.6 = (f32[128,960]{0,1:T(8,128)S(1)}, f32[128,960]{0,1:T(8,128)}, u32[]{:S(2)}) copy-start(f32[128,960]{0,1:T(8,128)} %copy-done.5) | copy-start | bytes 1474564
  (30 other events, 85.6 us)
Sparse Core Ops, SparseCore 0:
  81.5 23.5 all-gather.14
  107.3 83.5 all-gather.18
  193.0 44.2 all-gather.16
  239.3 55.5 all-gather.20
  296.8 55.9 all-gather.22
  354.8 55.9 all-gather.24
  974.4 69.0 all-reduce.4
